TPU v7x, 128 devices: a whole 4x4x4 slice. The times are simulated.
128 devices in a mesh: req: 8 (over y, core), hid: 16 (over x, z).
Axes of the slice: x: 4, y: 4, z: 4, core: 2. Of those that a mesh axis runs over, the one named last changes fastest.
Arguments:
- merged: bfloat16 [8, 256, 12800], P(None, 'req', 'hid')
- ln_gain: bfloat16 [12800], replicated, may hold values from 0.25 to 1.75
- ln_bias: bfloat16 [12800], replicated, may hold values from -3 to 3
- proj_weight: bfloat16 [12800, 6144], P(None, 'hid'), may hold values from -0.0546875 to 0.0546875
- proj_bias: float32 [6144], P('hid'), may hold values from -3 to 3
- text_embed: bfloat16 [16, 480, 6144], P('req', None, 'hid')
- attn_gain: bfloat16 [6144], replicated, may hold values from 0.25 to 1.75
- query_weight: bfloat16 [6144, 6144], P(None, 'hid')
- key_weight: bfloat16 [6144, 1024], P(None, 'hid')
- value_weight: bfloat16 [6144, 1024], P(None, 'hid'), may hold values from -0.078125 to 0.078125
- out_weight: bfloat16 [6144, 6144], P('hid'), may hold values from -0.078125 to 0.078125
- final_gain: bfloat16 [6144], replicated, may hold values from 0.25 to 1.75
- head_weight: bfloat16 [49152, 6144], P(('req', 'hid')), may hold values from -0.23925781 to 0.23925781
- lengths: int32 [16], P('req'), may hold values from 160 to 480, as said below
- tile_request: int32 [8], replicated, may hold values from 0 to 15, as said below
- insert_pos: int32 [8], replicated, may hold values from 0 to 224, as said below
Outputs:
- hidden: bfloat16 [16, 480, 6144], P('req', None, 'hid')
- final_norm: float32 [16], replicated
- logit_max: float32 [16], replicated
Inputs may be any that keep to these rules, and one draw needn't show every extreme that they name: For every g, the requests 2g and 2g + 1 have lengths that add up to exactly 640. `tile_request`: each pair of requests 2g, 2g + 1 holds exactly one tile, in the one of the two whose length is not smaller. insert_pos[t] + 256 is at most the length of request tile_request[t].
All inputs are finite; a program needn't handle non-finite values.
Results may differ from a plain program's by a relative error of at most 0.0095.
Values may be sent and summed in bfloat16 or wider, within the bound.
No kernel may reach another device: no remote copies, remote signals or barrier semaphores. Data moves between devices by JAX's collectives and lax.ppermute only.
A program may use at most 128 MiB of HBM per device.

v0:
```python
import math
import jax
import jax.numpy as jnp
from jax import lax
from jax.sharding import PartitionSpec as P

HEAD_DIM = 128
D = 6144
REQ_GRP = 2


def from_partner(block, axis, stride):
    count = lax.axis_size(axis)
    route = []
    for low in range(count):
        high = low | 1 << stride
        if high != low and high < count:
            route += [(low, high), (high, low)]
    return lax.ppermute(block, axis, route)


def rotary(values, positions):
    half_dim = values.shape[-1] // 2
    inv_freq = jnp.exp(
        jnp.arange(half_dim, dtype=jnp.float32) * (-2.0 * math.log(1000000.0) / values.shape[-1])
    )
    angles = positions.astype(jnp.float32)[:, None] * inv_freq[None, :]
    cosine = jnp.cos(angles)[:, None, :]
    sine_val = jnp.sin(angles)[:, None, :]
    first_half = values[..., :half_dim]
    second = values[..., half_dim:]
    return jnp.concatenate(
        [first_half * cosine - second * sine_val, second * cosine + first_half * sine_val], axis=-1
    )


def attend_local(queries, key_rows, value_rows, length):
    scores = jnp.einsum(
        "qhd,sd->hqs", queries, key_rows, preferred_element_type=jnp.float32
    ) / math.sqrt(HEAD_DIM)
    positions = jnp.arange(queries.shape[0])
    allowed = positions[None, :] <= positions[:, None]
    scores = jnp.where(allowed[None], scores, -jnp.inf)
    row_top = jnp.max(scores, axis=-1, keepdims=True)
    weights = jnp.exp(scores - row_top)
    weights = (weights / jnp.sum(weights, axis=-1, keepdims=True)).astype(jnp.bfloat16)
    mixed_out = jnp.einsum("hqs,sd->qhd", weights, value_rows, preferred_element_type=jnp.float32)
    mixed_out = jnp.where((positions < length)[:, None, None], mixed_out, 0.0)
    return mixed_out.reshape(queries.shape[0], -1).astype(jnp.bfloat16)


def shards(
    merged,
    ln_gain,
    ln_bias,
    proj_weight,
    proj_bias,
    text_embed,
    attn_gain,
    query_weight,
    key_weight,
    value_weight,
    out_weight,
    final_gain,
    head_weight,
    lengths,
    tile_request,
    insert_pos,
):
    owners = tile_request // REQ_GRP
    tile_order = jnp.argsort(owners)
    outgoing = merged[tile_order]
    arrived = lax.all_to_all(outgoing, "req", split_axis=0, concat_axis=1, tiled=True)
    features = lax.all_gather(arrived[0], "hid", axis=1, tiled=True)
    values = features.astype(jnp.float32)
    row_mean = jnp.mean(values, axis=1, keepdims=True)
    row_var = jnp.mean(values * values, axis=1, keepdims=True) - row_mean * row_mean
    normed = (
        (values - row_mean) * lax.rsqrt(row_var + 1e-05) * ln_gain.astype(jnp.float32)
        + ln_bias.astype(jnp.float32)
    ).astype(jnp.bfloat16)
    projected = jnp.dot(normed, proj_weight, preferred_element_type=jnp.float32) + proj_bias
    projected = jax.nn.gelu(projected, approximate=False).astype(jnp.bfloat16)
    own_tile = tile_order[lax.axis_index("req")]
    local_req = tile_request[own_tile] % REQ_GRP
    embedded = lax.dynamic_update_slice(
        text_embed, projected[None], (local_req, insert_pos[own_tile], jnp.zeros((), jnp.int32))
    )
    length_max = text_embed.shape[1]
    flat_rows = embedded.reshape(REQ_GRP * length_max, -1)
    position = jnp.arange(length_max)
    gain_part = attn_gain.astype(jnp.float32)
    portion_f = lax.all_gather(flat_rows, "hid", axis=1, tiled=True).astype(jnp.float32)
    scaled = (portion_f * gain_part).astype(jnp.bfloat16)
    squares = jnp.sum(portion_f * portion_f, axis=1)
    q_total = jnp.dot(scaled, query_weight, preferred_element_type=jnp.float32)
    k_total = jnp.dot(scaled, key_weight, preferred_element_type=jnp.float32)
    v_total = jnp.dot(scaled, value_weight, preferred_element_type=jnp.float32)
    row_scale = lax.rsqrt(squares / D + 1e-05)[:, None]
    queries = q_total * row_scale
    key_half = (k_total * row_scale).astype(jnp.bfloat16)
    value_half = (v_total * row_scale).astype(jnp.bfloat16)
    other_key, other_value = from_partner((key_half, value_half), "hid", 0)
    is_lower = lax.axis_index("hid") % 2 == 0
    key_raw = jnp.where(
        is_lower,
        jnp.concatenate([key_half, other_key], 1),
        jnp.concatenate([other_key, key_half], 1),
    )
    kv_values = jnp.where(
        is_lower,
        jnp.concatenate([value_half, other_value], 1),
        jnp.concatenate([other_value, value_half], 1),
    )
    heads_local = queries.shape[1] // HEAD_DIM
    queries = queries.reshape(REQ_GRP, length_max, heads_local, HEAD_DIM)
    key_raw = key_raw.reshape(REQ_GRP, length_max, 1, HEAD_DIM)
    kv_values = kv_values.reshape(REQ_GRP, length_max, HEAD_DIM)
    pieces = []
    for request in range(REQ_GRP):
        q_rotated = rotary(queries[request], position).astype(jnp.bfloat16)
        k_rotated = rotary(key_raw[request].astype(jnp.float32), position).astype(jnp.bfloat16)[
            :, 0, :
        ]
        pieces.append(attend_local(q_rotated, k_rotated, kv_values[request], lengths[request]))
    attended = jnp.concatenate(pieces, axis=0)
    partial_value = jnp.dot(attended, out_weight, preferred_element_type=jnp.float32)
    attn_sum = lax.psum_scatter(
        partial_value.astype(jnp.bfloat16), "hid", scatter_dimension=1, tiled=True
    ).astype(jnp.float32)
    hidden = (
        (flat_rows.astype(jnp.float32) + attn_sum)
        .astype(jnp.bfloat16)
        .reshape(REQ_GRP, length_max, -1)
    )
    last_rows = hidden[jnp.arange(REQ_GRP), lengths - 1]
    full_width = lax.all_gather(last_rows, "hid", axis=1, tiled=True)
    all_last = lax.all_gather(full_width, "req", axis=0, tiled=True)
    last_values = all_last.astype(jnp.float32)
    last_squares = jnp.sum(last_values * last_values, axis=1)
    final_norm = jnp.sqrt(last_squares)
    final_scaled = (
        last_values * lax.rsqrt(last_squares / D + 1e-05)[:, None] * final_gain.astype(jnp.float32)
    ).astype(jnp.bfloat16)
    logits = lax.dot_general(
        final_scaled, head_weight, (((1,), (1,)), ((), ())), preferred_element_type=jnp.float32
    )
    logit_max = lax.pmax(jnp.max(logits, axis=1), ("req", "hid"))
    return (hidden, final_norm, logit_max)


def solution(mesh):
    return jax.shard_map(
        shards,
        mesh=mesh,
        in_specs=(
            P(None, "req", "hid"),
            P(),
            P(),
            P(None, "hid"),
            P("hid"),
            P("req", None, "hid"),
            P(),
            P(None, "hid"),
            P(None, "hid"),
            P(None, "hid"),
            P("hid", None),
            P(),
            P(("req", "hid"), None),
            P("req"),
            P(),
            P(),
        ),
        out_specs=(P("req", None, "hid"), P(), P()),
        check_vma=False,
    )
```

profile of v0, /device:TPU:1, one launch (start us, length us, event | category | flops | bytes accessed | tf_op | source)
XLA Modules:
  0.0 486.7 jit_solution(6029854030120784377)
XLA Ops:
  7.2 0.7 and_select_fusion
  8.0 1.0 sort.17
  8.9 1.6 gather_fusion
  10.6 14.5 %all_to_all.4 = bf16[8,32,800]{2,1,0:T(8,128)(2,1)S(1)} all-to-all(bf16[8,32,800]{2,1,0:T(8,128)(2,1)S(1)} %gather_fusion), channel_id=1, replica_groups=mesh['req'=8,'hid'=16] {'req'}, dimensions={0} | all-to-all | bytes 819200 | tf_op jit(solution)/shard_map/all_to_all | solution.py:73
  25.1 0.9 copy.58
  26.1 0.0 all-gather.6.cloned.1.call-start
  26.1 0.6 dynamic_slice.9
  28.7 1.2 dynamic_slice.10
  31.9 1.2 dynamic_slice.11
  34.4 0.8 convert_element_type.138
  35.8 53.5 %all-gather.4.cloned.1.call-done = bf16[256,12800]{0,1:T(8,128)(2,1)} async-done(((bf16[256,800]{0,1:T(8,128)(2,1)}), bf16[256,12800]{0,1:T(8,128)(2,1)}) %all-gather.4.cloned.1.call-update) | async-done | bytes 6553616 | tf_op jit(solution)/shard_map/all_gather | solution.py:74
  89.4 4.9 %convert_reduce_fusion = (f32[256]{0:T(256)S(1)}, f32[256]{0:T(256)S(1)}) fusion(bf16[256,12800]{0,1:T(8,128)(2,1)} %all-gather.4.cloned.1.call-done), kind=kLoop, calls=%fused_computation.10 | loop fusion | flops 13106688 | bytes 6555648 | tf_op jit(solution)/shard_map/reduce_sum | solution.py:76
  94.3 15.5 %fusion.70 = bf16[1,256,384]{2,1,0:T(8,128)(2,1)S(1)} fusion(bf16[12800,384]{1,0:T(8,128)(2,1)} %param.19, bf16[256,12800]{0,1:T(8,128)(2,1)S(1)} %copy-done.6, f32[12800]{0:T(1024)S(1)} %convert_element_type.139, f32[12800]{0:T(1024)S(1)} %convert_element_type.138, f32[256]{0:T(256)S(1)} %get-tuple-element.30, f32[256]{0:T(256)S(1)} %get-tuple-element.29, ...), kind=kOutput, calls=%fused_computation.84 | convolution fusion | flops 2542731264 | bytes 16686592 | tf_op jit(solution)/shard_map/dot_general | solution.py:82
  109.9 1.4 dynamic_update_slice.3
  111.3 0.9 copy-done.3
  112.2 0.0 reduce-scatter.4.cloned.1.call-start
  112.3 0.6 fusion.121
  113.0 1.2 iota_compare_fusion.2
  114.2 1.2 iota_compare_fusion.1
  115.4 0.8 iota_compare_fusion
  116.2 1.7 multiply_cosine_fusion
  117.9 88.9 %all-gather.6.cloned.1.call-done = bf16[960,6144]{1,0:T(8,128)(2,1)} async-done(((bf16[960,384]{1,0:T(8,128)(2,1)}), bf16[960,6144]{1,0:T(8,128)(2,1)}) %all-gather.6.cloned.1.call-update) | async-done | bytes 11796496 | tf_op jit(solution)/shard_map/all_gather | solution.py:93
  206.8 6.8 %fusion.3 = f32[960]{0:T(1024)S(1)} fusion(bf16[960,6144]{1,0:T(8,128)(2,1)} %all-gather.6.cloned.1.call-done), kind=kLoop, calls=%fused_computation.7 | loop fusion | flops 17693760 | bytes 11800320 | tf_op jit(solution)/shard_map/reduce_sum | solution.py:95
  213.6 8.1 %fusion.52 = bf16[960,64]{0,1:T(8,128)(2,1)S(1)} fusion(bf16[6144,64]{0,1:T(8,128)(2,1)S(1)} %copy-done, bf16[960,6144]{1,0:T(8,128)(2,1)} %all-gather.6.cloned.1.call-done, f32[6144]{0:T(1024)S(1)} %convert_element_type.144, f32[960]{0:T(1024)S(1)} %add_rsqrt_fusion), kind=kOutput, calls=%fused_computation.53 | convolution fusion | flops 772792320 | bytes 12734208 | tf_op jit(solution)/shard_map/dot_general | solution.py:97
  221.8 1.1 collective-permute-start.1
  222.9 6.3 %fusion.23 = f32[960,384]{1,0:T(8,128)S(1)} fusion(bf16[6144,384]{1,0:T(8,128)(2,1)S(1)} %bitcast.98, bf16[960,6144]{1,0:T(8,128)(2,1)S(1)} %copy-done.2, f32[6144]{0:T(1024)S(1)} %convert_element_type.144, f32[960]{0:T(1024)S(1)} %add_rsqrt_fusion), kind=kOutput, calls=%fused_computation.33 | convolution fusion | flops 4547911680 | bytes 18018048 | tf_op jit(solution)/shard_map/dot_general | solution.py:96
  229.2 0.1 fusion.118
  229.3 0.3 copy.59
  229.5 0.1 fusion.119
  229.6 0.3 copy.85
  229.9 0.3 copy.86
  230.2 0.3 copy.66
  230.4 0.1 fusion.120
  230.5 0.3 copy.87
  230.8 0.3 copy.88
  231.1 8.2 %fusion.46 = bf16[960,64]{0,1:T(8,128)(2,1)S(1)} fusion(bf16[6144,64]{0,1:T(8,128)(2,1)} %param.25, bf16[960,6144]{1,0:T(8,128)(2,1)} %all-gather.6.cloned.1.call-done, f32[6144]{0:T(1024)S(1)} %convert_element_type.144, f32[960]{0:T(1024)S(1)} %add_rsqrt_fusion), kind=kOutput, calls=%fused_computation.51 | convolution fusion | flops 772792320 | bytes 12734208 | tf_op jit(solution)/shard_map/dot_general | solution.py:98
  239.2 0.9 collective-permute-start
  240.2 1.1 subtract_convert_fusion.1
  241.3 1.0 maximum_select_fusion.1
  242.3 0.1 fusion.100
  242.4 0.6 fusion.108
  243.0 0.6 fusion.73
  243.7 1.5 fusion.123
  245.3 0.1 maximum_select_fusion
  245.3 0.8 fusion.41
  246.2 0.2 copy.65
  246.4 0.6 fusion.77
  247.0 1.5 fusion.122
  248.6 0.8 fusion.42
  249.4 0.2 copy.72
  249.6 12.0 %convolution_convert_fusion = bf16[960,6144]{1,0:T(8,128)(2,1)} fusion(bf16[384,6144]{1,0:T(8,128)(2,1)} %param.26, bf16[480,384]{0,1:T(8,128)(2,1)S(1)} %bitcast.92, bf16[480,384]{0,1:T(8,128)(2,1)S(1)} %bitcast.91), kind=kOutput, calls=%fused_computation.16 | convolution fusion | flops 4537221120 | bytes 17252352 | tf_op jit(solution)/shard_map/dot_general | solution.py:127
  261.6 16.4 %copy.83 = bf16[960,6144]{0,1:T(8,128)(2,1)} copy(bf16[960,6144]{1,0:T(8,128)(2,1)} %convolution_convert_fusion) | data formatting | bytes 23592960
  278.1 0.7 copy-done.15
  278.8 94.4 %reduce-scatter.4.cloned.1.call-done = bf16[384,960]{1,0:T(8,128)(2,1)} async-done(((bf16[6144,960]{1,0:T(8,128)(2,1)}), bf16[384,960]{1,0:T(8,128)(2,1)}) %reduce-scatter.4.cloned.1.call-update) | async-done | bytes 737296
  373.2 1.6 copy.84
  374.8 0.3 add_convert_fusion
  375.0 0.6 gather_fusion.1
  375.7 15.8 %all_gather.14 = bf16[2,6144]{1,0:T(2,128)(2,1)S(1)} all-gather(bf16[2,384]{1,0:T(2,128)(2,1)S(1)} %gather_fusion.1), channel_id=1, replica_groups=mesh['req'=8,'hid'=16] {'hid'}, dimensions={1}, use_global_device_ids=true | all-gather | bytes 26112 | tf_op jit(solution)/shard_map/all_gather | solution.py:137
  391.5 20.4 %all-gather = bf16[8,2,6144]{2,1,0:T(2,128)(2,1)S(1)} all-gather(bf16[1,2,6144]{2,1,0:T(2,128)(2,1)S(1)} %bitcast.96), channel_id=1, replica_groups=mesh['req'=8,'hid'=16] {'req'}, dimensions={0}, use_global_device_ids=true | all-gather | bytes 221184 | tf_op jit(solution)/shard_map/all_gather | solution.py:138
  411.8 0.1 reshape.250
  411.9 0.2 multiply_reduce_fusion
  412.1 0.5 add_rsqrt_fusion.2
  412.6 3.8 convolution_reduce_fusion
  416.4 63.8 %pmax.7 = f32[16]{0:T(128)} all-reduce(f32[16]{0:T(128)S(1)} %convolution_reduce_fusion), channel_id=1, replica_groups=mesh['req'=8,'hid'=16] {'req','hid'}, use_global_device_ids=true, to_apply=%region_11.12 | all-reduce | flops 16 | bytes 128 | tf_op jit(solution)/shard_map/pmax | solution.py:148
  (66 shorter events, 0.3 us)
Async XLA Ops:
  7.2 206.4 %copy-start = (bf16[6144,64]{0,1:T(8,128)(2,1)S(1)}, bf16[6144,64]{0,1:T(8,128)(2,1)}, u32[]{:S(2)}) copy-start(bf16[6144,64]{0,1:T(8,128)(2,1)} %param.24) | copy-start | bytes 2359300
  7.2 28.0 %copy-start.13 = (bf16[12800]{0:T(1024)(128)(2,1)S(1)}, bf16[12800]{0:T(1024)(128)(2,1)}, u32[]{:S(2)}) copy-start(bf16[12800]{0:T(1024)(128)(2,1)} %param.18) | copy-start | bytes 76804
  7.2 82.2 %all-gather.4.cloned.1.call-start = ((), (), s32[]{:S(2)}) async-start(), calls=%async_computation.2 | async-start | bytes 6963200 | tf_op jit(solution)/shard_map/all_gather | solution.py:74
  10.6 83.7 %copy-start.20 = (f32[384]{0:T(512)S(1)}, f32[384]{0:T(512)}, u32[]{:S(2)}) copy-start(f32[384]{0:T(512)} %param.20) | copy-start | bytes 4612
  26.1 180.7 %all-gather.6.cloned.1.call-start = ((), (), s32[]{:S(2)}) async-start(), calls=%async_computation.3 | async-start | bytes 12533760 | tf_op jit(solution)/shard_map/all_gather | solution.py:93
  89.4 4.9 %copy-start.6 = (bf16[256,12800]{0,1:T(8,128)(2,1)S(1)}, bf16[256,12800]{0,1:T(8,128)(2,1)}, u32[]{:S(2)}) copy-start(bf16[256,12800]{0,1:T(8,128)(2,1)} %all-gather.4.cloned.1.call-done) | copy-start | bytes 19660804
  94.3 15.6 %copy-start.5 = (bf16[2,480,384]{2,1,0:T(8,128)(2,1)S(1)}, bf16[2,480,384]{2,1,0:T(8,128)(2,1)}, u32[]{:S(2)}) copy-start(bf16[2,480,384]{2,1,0:T(8,128)(2,1)} %param.21) | copy-start | bytes 2211844
  94.3 18.0 %copy-start.14 = (bf16[6144]{0:T(1024)(128)(2,1)S(1)}, bf16[6144]{0:T(1024)(128)(2,1)}, u32[]{:S(2)}) copy-start(bf16[6144]{0:T(1024)(128)(2,1)} %param.22) | copy-start | bytes 36868
  94.3 18.0 %copy-start.16 = (s32[2]{0:T(128)S(1)}, s32[2]{0:T(128)}, u32[]{:S(2)}) copy-start(s32[2]{0:T(128)} %param.29) | copy-start | bytes 28
  111.3 0.9 copy-start.3
  112.2 260.9 %reduce-scatter.4.cloned.1.call-start = ((), (), s32[]{:S(2)}) async-start(), calls=%async_computation.4 | async-start | bytes 13369344
  112.3 101.2 %copy-start.18 = (f32[64]{0:T(128)}, f32[64]{0:T(128)S(1)}, u32[]{:S(2)}) copy-start(f32[64]{0:T(128)S(1)} %multiply_exponential_fusion) | copy-start | bytes 772
  206.8 16.1 %slice-start = ((s8[4718592]{0:T(1024)(128)(4,1)}), s8[524288]{0:T(1024)(128)(4,1)S(1)}, s32[]{:S(2)}) async-start(s8[4718592]{0:T(1024)(128)(4,1)} %bitcast.97), calls=%async_computation.5 | async-start | bytes 1048576
  213.6 9.3 %copy-start.2 = (bf16[960,6144]{1,0:T(8,128)(2,1)S(1)}, bf16[960,6144]{1,0:T(8,128)(2,1)}, u32[]{:S(2)}) copy-start(bf16[960,6144]{1,0:T(8,128)(2,1)} %all-gather.6.cloned.1.call-done) | copy-start | bytes 35389444
  213.6 9.3 %slice-start.1 = ((s8[4718592]{0:T(1024)(128)(4,1)}), s8[4194304]{0:T(1024)(128)(4,1)S(1)}, s32[]{:S(2)}) async-start(s8[4718592]{0:T(1024)(128)(4,1)} %bitcast.97), calls=%async_computation.6 | async-start | bytes 8388608
  221.8 19.5 %collective-permute-start.1 = (bf16[960,64]{0,1:T(8,128)(2,1)S(1)}, bf16[960,64]{0,1:T(8,128)(2,1)}, u32[]{:S(2)}, u32[]{:S(2)}) collective-permute-start(bf16[960,64]{0,1:T(8,128)(2,1)S(1)} %fusion.52), channel_id=1, source_target_pairs={{0,1},{1,0},{2,3},{3,2},{4,5},{5,4},{6,7},{7,6},{8,9},{9,8},{10,11... | collective-permute-start | bytes 368648 | tf_op jit(solution)/shard_map/ppermute | solution.py:19
  231.0 9.1 %copy-start.8 = (f32[480,64]{1,0:T(8,128)S(1)}, f32[480,64]{1,0:T(8,128)}, u32[]{:S(2)}) copy-start(f32[480,64]{1,0:T(8,128)} %get-tuple-element.27) | copy-start | bytes 368644
  231.0 9.1 %copy-start.9 = (f32[480,64]{1,0:T(8,128)S(1)}, f32[480,64]{1,0:T(8,128)}, u32[]{:S(2)}) copy-start(f32[480,64]{1,0:T(8,128)} %get-tuple-element.28) | copy-start | bytes 368644
  239.2 3.2 copy-start.19
  239.2 6.0 %collective-permute-start = (bf16[960,64]{0,1:T(8,128)(2,1)S(1)}, bf16[960,64]{0,1:T(8,128)(2,1)S(1)}, u32[]{:S(2)}, u32[]{:S(2)}) collective-permute-start(bf16[960,64]{0,1:T(8,128)(2,1)S(1)} %fusion.46), channel_id=1, source_target_pairs={{0,1},{1,0},{2,3},{3,2},{4,5},{5,4},{6,7},{7,6},{8,9},{9,8},{10,11... | collective-permute-start | bytes 368648 | tf_op jit(solution)/shard_map/ppermute | solution.py:19
  240.1 3.5 copy-start.11
  243.7 1.6 copy-start.22
  245.3 1.0 copy-start.7
  245.3 1.7 copy-start.12
  246.3 2.2 copy-start.21
  278.1 0.7 copy-start.15
  278.1 0.7 copy-start.17
  278.1 96.7 %copy-start.4 = (bf16[2,480,384]{2,1,0:T(8,128)(2,1)S(1)}, bf16[2,480,384]{2,1,0:T(8,128)(2,1)}, u32[]{:S(2)}) copy-start(bf16[2,480,384]{2,1,0:T(8,128)(2,1)} %copy-done.3) | copy-start | bytes 2211844
  373.2 107.0 %copy-start.1 = (bf16[6144,64]{0,1:T(8,128)(2,1)S(1)}, bf16[6144,64]{0,1:T(8,128)(2,1)}, u32[]{:S(2)}) copy-start(bf16[6144,64]{0,1:T(8,128)(2,1)} %param.24) | copy-start | bytes 2359300
  375.0 105.1 %copy-start.10 = (bf16[960,384]{1,0:T(8,128)(2,1)}, bf16[960,384]{1,0:T(8,128)(2,1)S(1)}, u32[]{:S(2)}) copy-start(bf16[960,384]{1,0:T(8,128)(2,1)S(1)} %add_convert_fusion) | copy-start | bytes 2211844
Sparse Core Ops, SparseCore 0:
  26.2 63.1 all-gather.3
  112.3 94.4 all-gather.5
  278.2 94.9 reduce-scatter.3
where the time goes:
time: 488 us; the launch traced here: 487 us
  waiting for transfers between devices  237 us (49%)
  blocking collectives  114 us (23%)
  matrix products  56.8 us (12%)
  local copies, waits for them, and re-layouts  30.2 us (6%)
  other arithmetic  26 us (5%)
  between operations  20.1 us (4%)
    unnamed x4, waiting for transfers between devices  94.4 us
    all_gather x1, waiting for transfers between devices, shards(): lax.all_gather(flat_rows, 'hid', axis=1, tiled=True).astype(jnp.float32)  88.9 us
    pmax x1, blocking collectives, shards(): logit_max = lax.pmax(jnp.max(logits, axis=1), ('req', 'hid'))  63.8 us
    all_gather x1, waiting for transfers between devices, shards(): features = lax.all_gather(arrived[0], 'hid', axis=1, tiled=True)  53.5 us
    unnamed x56, local copies, waits for them, and re-layouts  20.7 us
    all_gather x1, blocking collectives, shards(): all_last = lax.all_gather(full_width, 'req', axis=0, tiled=True)  20.4 us
    all_gather x1, blocking collectives, shards(): full_width = lax.all_gather(last_rows, 'hid', axis=1, tiled=True)  15.8 us
    dot_general x1, matrix products, shards(): jnp.dot(normed, proj_weight, preferred_element_type=jnp.float32) + proj_bias  15.5 us
  transfers between devices with their start and end apart: 5, of which 3 were waited for; matrix products, arithmetic and copies ran while one was open for 6% of the time, Pallas kernels for 0%

commit v1 on v0

--- a/solution.py
+++ b/solution.py
@@ -135,7 +135,13 @@
     )
     last_rows = hidden[jnp.arange(REQ_GRP), lengths - 1]
     full_width = lax.all_gather(last_rows, "hid", axis=1, tiled=True)
-    all_last = lax.all_gather(full_width, "req", axis=0, tiled=True)
+    size = lax.axis_size("req")
+    held, blocks = (full_width, [full_width])
+    for _ in range(size - 1):
+        held = lax.ppermute(held, "req", [(i, (i + 1) % size) for i in range(size)])
+        blocks.insert(0, held)
+    line = jnp.concatenate(blocks, axis=0)
+    all_last = jnp.roll(line, (lax.axis_index("req") + 1) * full_width.shape[0], axis=0)
     last_values = all_last.astype(jnp.float32)
     last_squares = jnp.sum(last_values * last_values, axis=1)
     final_norm = jnp.sqrt(last_squares)

time: 488 us -> 505 us (1.035)
  waiting for transfers between devices: 237 us -> 258 us
  blocking collectives: 114 us -> 95.8 us
  starting transfers between devices: 2.14 us -> 16.6 us
    ppermute x0 -> x7, waiting for transfers between devices: none -> 20.5 us  [shards(): held = lax.ppermute(held, 'req', [(i, (i + 1) % size) for i in range(size)])]
    all_gather x1 -> x0, blocking collectives: 20.4 us -> none  [shards(): all_last = lax.all_gather(full_width, 'req', axis=0, tiled=True)]
    ppermute x0 -> x7, starting transfers between devices: none -> 14.4 us  [shards(): held = lax.ppermute(held, 'req', [(i, (i + 1) % size) for i in range(size)])]
  transfers between devices with their start and end apart: 5 -> 12, of which waited for: 3 -> 10; matrix products, arithmetic and copies ran while one was open for 6% -> 6% of each run, Pallas kernels for 0% -> 0%
where the time goes in v1:
time: 505 us; the launch traced here: 504 us
  waiting for transfers between devices  258 us (51%)
  blocking collectives  95.8 us (19%)
  matrix products  56.8 us (11%)
  local copies, waits for them, and re-layouts  30.7 us (6%)
  other arithmetic  26 us (5%)
  between operations  20.2 us (4%)
  starting transfers between devices  16.6 us (3%)
    unnamed x4, waiting for transfers between devices  94.9 us
    all_gather x1, waiting for transfers between devices, shards(): lax.all_gather(flat_rows, 'hid', axis=1, tiled=True).astype(jnp.float32)  88.9 us
    pmax x1, blocking collectives, shards(): logit_max = lax.pmax(jnp.max(logits, axis=1), ('req', 'hid'))  65.5 us
    all_gather x1, waiting for transfers between devices, shards(): features = lax.all_gather(arrived[0], 'hid', axis=1, tiled=True)  53.5 us
    unnamed x56, local copies, waits for them, and re-layouts  20.6 us
    ppermute x7, waiting for transfers between devices, shards(): held = lax.ppermute(held, 'req', [(i, (i + 1) % size) for i in range(size)])  20.5 us
    all_gather x1, blocking collectives, shards(): full_width = lax.all_gather(last_rows, 'hid', axis=1, tiled=True)  15.8 us
    dot_general x1, matrix products, shards(): jnp.dot(normed, proj_weight, preferred_element_type=jnp.float32) + proj_bias  15.5 us
  transfers between devices with their start and end apart: 12, of which 10 were waited for; matrix products, arithmetic and copies ran while one was open for 6% of the time, Pallas kernels for 0%

profile of v1, /device:TPU:1, one launch (start us, length us, event | category | flops | bytes accessed | tf_op | source)
XLA Modules:
  0.0 503.9 jit_solution(2974722237319108766)
XLA Ops:
  7.2 0.7 and_select_fusion
  8.0 1.0 sort.17
  8.9 1.6 gather_fusion
  10.6 14.5 %all_to_all.4 = bf16[8,32,800]{2,1,0:T(8,128)(2,1)S(1)} all-to-all(bf16[8,32,800]{2,1,0:T(8,128)(2,1)S(1)} %gather_fusion), channel_id=1, replica_groups=mesh['req'=8,'hid'=16] {'req'}, dimensions={0} | all-to-all | bytes 819200 | tf_op jit(solution)/shard_map/all_to_all | solution.py:73
  25.1 0.9 copy.58
  26.1 0.6 dynamic_slice.13
  28.7 1.2 dynamic_slice.14
  31.9 1.2 dynamic_slice.15
  34.4 0.8 convert_element_type.138
  35.8 53.5 %all-gather.3.cloned.1.call-done = bf16[256,12800]{0,1:T(8,128)(2,1)} async-done(((bf16[256,800]{0,1:T(8,128)(2,1)}), bf16[256,12800]{0,1:T(8,128)(2,1)}) %all-gather.3.cloned.1.call-update) | async-done | bytes 6553616 | tf_op jit(solution)/shard_map/all_gather | solution.py:74
  89.4 4.9 convert_reduce_fusion
  94.3 15.5 %fusion.73 = bf16[1,256,384]{2,1,0:T(8,128)(2,1)S(1)} fusion(bf16[12800,384]{1,0:T(8,128)(2,1)} %param.19, bf16[256,12800]{0,1:T(8,128)(2,1)S(1)} %copy-done.6, f32[12800]{0:T(1024)S(1)} %convert_element_type.139, f32[12800]{0:T(1024)S(1)} %convert_element_type.138, f32[256]{0:T(256)S(1)} %get-tuple-element.30, f32[256]{0:T(256)S(1)} %get-tuple-element.29, ...), kind=kOutput, calls=%fused_computation.87 | convolution fusion | flops 2542731264 | bytes 16686592 | tf_op jit(solution)/shard_map/dot_general | solution.py:82
  109.9 1.4 dynamic_update_slice.3
  111.3 0.9 copy-done.3
  112.3 0.7 fusion.127
  113.0 1.2 iota_compare_fusion.2
  114.2 1.2 iota_compare_fusion.1
  115.4 0.8 iota_compare_fusion
  116.2 1.7 multiply_cosine_fusion
  117.9 88.9 %all-gather.5.cloned.1.call-done = bf16[960,6144]{1,0:T(8,128)(2,1)} async-done(((bf16[960,384]{1,0:T(8,128)(2,1)}), bf16[960,6144]{1,0:T(8,128)(2,1)}) %all-gather.5.cloned.1.call-update) | async-done | bytes 11796496 | tf_op jit(solution)/shard_map/all_gather | solution.py:93
  206.8 6.8 %fusion.3 = f32[960]{0:T(1024)S(1)} fusion(bf16[960,6144]{1,0:T(8,128)(2,1)} %all-gather.5.cloned.1.call-done), kind=kLoop, calls=%fused_computation.7 | loop fusion | flops 17693760 | bytes 11800320 | tf_op jit(solution)/shard_map/reduce_sum | solution.py:95
  213.6 8.1 %fusion.52 = bf16[960,64]{0,1:T(8,128)(2,1)S(1)} fusion(bf16[6144,64]{0,1:T(8,128)(2,1)S(1)} %copy-done, bf16[960,6144]{1,0:T(8,128)(2,1)} %all-gather.5.cloned.1.call-done, f32[6144]{0:T(1024)S(1)} %convert_element_type.144, f32[960]{0:T(1024)S(1)} %add_rsqrt_fusion), kind=kOutput, calls=%fused_computation.53 | convolution fusion | flops 772792320 | bytes 12734208 | tf_op jit(solution)/shard_map/dot_general | solution.py:97
  221.8 1.1 collective-permute-start.1
  222.9 6.3 %fusion.23 = f32[960,384]{1,0:T(8,128)S(1)} fusion(bf16[6144,384]{1,0:T(8,128)(2,1)S(1)} %bitcast.96, bf16[960,6144]{1,0:T(8,128)(2,1)S(1)} %copy-done.2, f32[6144]{0:T(1024)S(1)} %convert_element_type.144, f32[960]{0:T(1024)S(1)} %add_rsqrt_fusion), kind=kOutput, calls=%fused_computation.33 | convolution fusion | flops 4547911680 | bytes 18018048 | tf_op jit(solution)/shard_map/dot_general | solution.py:96
  229.3 0.3 copy.59
  229.6 0.3 copy.85
  229.9 0.3 copy.86
  230.2 0.3 copy.66
  230.5 0.3 copy.87
  230.8 0.3 copy.88
  231.1 8.2 %fusion.46 = bf16[960,64]{0,1:T(8,128)(2,1)S(1)} fusion(bf16[6144,64]{0,1:T(8,128)(2,1)} %param.25, bf16[960,6144]{1,0:T(8,128)(2,1)} %all-gather.5.cloned.1.call-done, f32[6144]{0:T(1024)S(1)} %convert_element_type.144, f32[960]{0:T(1024)S(1)} %add_rsqrt_fusion), kind=kOutput, calls=%fused_computation.51 | convolution fusion | flops 772792320 | bytes 12734208 | tf_op jit(solution)/shard_map/dot_general | solution.py:98
  239.2 0.9 collective-permute-start
  240.2 1.1 subtract_convert_fusion.1
  241.3 1.0 maximum_select_fusion.1
  242.5 0.6 fusion.113
  243.1 0.6 fusion.76
  243.7 1.5 fusion.129
  245.4 0.8 fusion.41
  246.4 0.6 fusion.80
  247.0 1.5 fusion.128
  248.6 0.8 fusion.42
  249.6 12.0 %convolution_convert_fusion = bf16[960,6144]{1,0:T(8,128)(2,1)} fusion(bf16[384,6144]{1,0:T(8,128)(2,1)} %param.26, bf16[480,384]{0,1:T(8,128)(2,1)S(1)} %bitcast.91, bf16[480,384]{0,1:T(8,128)(2,1)S(1)} %bitcast.90), kind=kOutput, calls=%fused_computation.16 | convolution fusion | flops 4537221120 | bytes 17252352 | tf_op jit(solution)/shard_map/dot_general | solution.py:127
  261.6 16.4 %copy.83 = bf16[960,6144]{0,1:T(8,128)(2,1)} copy(bf16[960,6144]{1,0:T(8,128)(2,1)} %convolution_convert_fusion) | data formatting | bytes 23592960
  278.0 0.6 copy-done.17
  278.7 94.9 %reduce-scatter.4.cloned.1.call-done = bf16[384,960]{1,0:T(8,128)(2,1)} async-done(((bf16[6144,960]{1,0:T(8,128)(2,1)}), bf16[384,960]{1,0:T(8,128)(2,1)}) %reduce-scatter.4.cloned.1.call-update) | async-done | bytes 737296
  373.6 1.6 copy.84
  375.2 0.3 add_convert_fusion
  375.4 0.6 gather_fusion.1
  376.1 15.8 %all_gather.11 = bf16[2,6144]{1,0:T(2,128)(2,1)S(1)} all-gather(bf16[2,384]{1,0:T(2,128)(2,1)S(1)} %gather_fusion.1), channel_id=1, replica_groups=mesh['req'=8,'hid'=16] {'hid'}, dimensions={1}, use_global_device_ids=true | all-gather | bytes 26112 | tf_op jit(solution)/shard_map/all_gather | solution.py:137
  391.8 8.5 %collective-permute-start.2 = (bf16[2,6144]{1,0:T(2,128)(2,1)S(1)}, bf16[2,6144]{1,0:T(2,128)(2,1)S(1)}, u32[]{:S(2)}, u32[]{:S(2)}) collective-permute-start(bf16[2,6144]{1,0:T(2,128)(2,1)S(1)} %all_gather.11), channel_id=1, source_target_pairs={{0,16},{16,32},{32,48},{48,64},{64,80},{80,96},{96,112},{112,0},{1... | collective-permute-start | bytes 73736 | tf_op jit(solution)/shard_map/ppermute | solution.py:141
  400.3 0.9 collective-permute-done.2
  401.3 2.3 collective-permute-start.3
  403.6 0.9 collective-permute-done.3
  404.5 2.3 collective-permute-start.4
  406.9 2.0 collective-permute-done.4
  408.9 1.2 collective-permute-start.5
  410.1 3.2 collective-permute-done.5
  413.4 4.4 collective-permute-done.6
  417.8 4.5 collective-permute-done.7
  422.3 4.4 collective-permute-done.8
  426.7 0.6 concatenate.68
  427.5 0.5 add_rsqrt_fusion.2
  428.0 3.8 convolution_reduce_fusion
  431.8 65.5 %pmax.7 = f32[16]{0:T(128)} all-reduce(f32[16]{0:T(128)S(1)} %convolution_reduce_fusion), channel_id=1, replica_groups=mesh['req'=8,'hid'=16] {'req','hid'}, use_global_device_ids=true, to_apply=%region_11.12 | all-reduce | flops 16 | bytes 128 | tf_op jit(solution)/shard_map/pmax | solution.py:154
  (79 shorter events, 1.4 us)
Async XLA Ops:
  7.2 206.5 %copy-start = (bf16[6144,64]{0,1:T(8,128)(2,1)S(1)}, bf16[6144,64]{0,1:T(8,128)(2,1)}, u32[]{:S(2)}) copy-start(bf16[6144,64]{0,1:T(8,128)(2,1)} %param.24) | copy-start | bytes 2359300
  7.2 28.0 %copy-start.13 = (bf16[12800]{0:T(1024)(128)(2,1)S(1)}, bf16[12800]{0:T(1024)(128)(2,1)}, u32[]{:S(2)}) copy-start(bf16[12800]{0:T(1024)(128)(2,1)} %param.18) | copy-start | bytes 76804
  7.2 82.2 %all-gather.3.cloned.1.call-start = ((), (), s32[]{:S(2)}) async-start(), calls=%async_computation.2 | async-start | bytes 6963200 | tf_op jit(solution)/shard_map/all_gather | solution.py:74
  10.6 83.7 %copy-start.20 = (f32[384]{0:T(512)S(1)}, f32[384]{0:T(512)}, u32[]{:S(2)}) copy-start(f32[384]{0:T(512)} %param.20) | copy-start | bytes 4612
  26.1 180.7 %all-gather.5.cloned.1.call-start = ((), (), s32[]{:S(2)}) async-start(), calls=%async_computation.3 | async-start | bytes 12533760 | tf_op jit(solution)/shard_map/all_gather | solution.py:93
  89.4 4.9 copy-start.6
  94.3 15.6 %copy-start.5 = (bf16[2,480,384]{2,1,0:T(8,128)(2,1)S(1)}, bf16[2,480,384]{2,1,0:T(8,128)(2,1)}, u32[]{:S(2)}) copy-start(bf16[2,480,384]{2,1,0:T(8,128)(2,1)} %param.21) | copy-start | bytes 2211844
  94.3 18.0 %copy-start.14 = (bf16[6144]{0:T(1024)(128)(2,1)S(1)}, bf16[6144]{0:T(1024)(128)(2,1)}, u32[]{:S(2)}) copy-start(bf16[6144]{0:T(1024)(128)(2,1)} %param.22) | copy-start | bytes 36868
  94.3 18.0 %copy-start.16 = (s32[2]{0:T(128)S(1)}, s32[2]{0:T(128)}, u32[]{:S(2)}) copy-start(s32[2]{0:T(128)} %param.29) | copy-start | bytes 28
  111.3 0.9 copy-start.3
  112.2 261.4 %reduce-scatter.4.cloned.1.call-start = ((), (), s32[]{:S(2)}) async-start(), calls=%async_computation.4 | async-start | bytes 13369344
  112.3 101.3 %copy-start.18 = (f32[64]{0:T(128)}, f32[64]{0:T(128)S(1)}, u32[]{:S(2)}) copy-start(f32[64]{0:T(128)S(1)} %multiply_exponential_fusion) | copy-start | bytes 772
  206.8 16.1 %slice-start = ((s8[4718592]{0:T(1024)(128)(4,1)}), s8[524288]{0:T(1024)(128)(4,1)S(1)}, s32[]{:S(2)}) async-start(s8[4718592]{0:T(1024)(128)(4,1)} %bitcast.95), calls=%async_computation.5 | async-start | bytes 1048576
  213.6 9.3 %copy-start.2 = (bf16[960,6144]{1,0:T(8,128)(2,1)S(1)}, bf16[960,6144]{1,0:T(8,128)(2,1)}, u32[]{:S(2)}) copy-start(bf16[960,6144]{1,0:T(8,128)(2,1)} %all-gather.5.cloned.1.call-done) | copy-start | bytes 35389444
  213.6 9.3 %slice-start.1 = ((s8[4718592]{0:T(1024)(128)(4,1)}), s8[4194304]{0:T(1024)(128)(4,1)S(1)}, s32[]{:S(2)}) async-start(s8[4718592]{0:T(1024)(128)(4,1)} %bitcast.95), calls=%async_computation.6 | async-start | bytes 8388608
  221.8 19.5 %collective-permute-start.1 = (bf16[960,64]{0,1:T(8,128)(2,1)S(1)}, bf16[960,64]{0,1:T(8,128)(2,1)}, u32[]{:S(2)}, u32[]{:S(2)}) collective-permute-start(bf16[960,64]{0,1:T(8,128)(2,1)S(1)} %fusion.52), channel_id=1, source_target_pairs={{0,1},{1,0},{2,3},{3,2},{4,5},{5,4},{6,7},{7,6},{8,9},{9,8},{10,11... | collective-permute-start | bytes 368648 | tf_op jit(solution)/shard_map/ppermute | solution.py:19
  231.1 9.1 %copy-start.8 = (f32[480,64]{1,0:T(8,128)S(1)}, f32[480,64]{1,0:T(8,128)}, u32[]{:S(2)}) copy-start(f32[480,64]{1,0:T(8,128)} %get-tuple-element.27) | copy-start | bytes 368644
  231.1 9.1 %copy-start.9 = (f32[480,64]{1,0:T(8,128)S(1)}, f32[480,64]{1,0:T(8,128)}, u32[]{:S(2)}) copy-start(f32[480,64]{1,0:T(8,128)} %get-tuple-element.28) | copy-start | bytes 368644
  239.2 3.2 copy-start.19
  239.2 6.0 %collective-permute-start = (bf16[960,64]{0,1:T(8,128)(2,1)S(1)}, bf16[960,64]{0,1:T(8,128)(2,1)S(1)}, u32[]{:S(2)}, u32[]{:S(2)}) collective-permute-start(bf16[960,64]{0,1:T(8,128)(2,1)S(1)} %fusion.46), channel_id=1, source_target_pairs={{0,1},{1,0},{2,3},{3,2},{4,5},{5,4},{6,7},{7,6},{8,9},{9,8},{10,11... | collective-permute-start | bytes 368648 | tf_op jit(solution)/shard_map/ppermute | solution.py:19
  240.2 3.5 copy-start.11
  243.7 1.6 copy-start.22
  245.3 1.0 copy-start.7
  245.3 1.7 copy-start.12
  246.4 2.2 copy-start.21
  278.0 0.7 copy-start.17
  278.0 97.1 %copy-start.4 = (bf16[2,480,384]{2,1,0:T(8,128)(2,1)S(1)}, bf16[2,480,384]{2,1,0:T(8,128)(2,1)}, u32[]{:S(2)}) copy-start(bf16[2,480,384]{2,1,0:T(8,128)(2,1)} %copy-done.3) | copy-start | bytes 2211844
  278.0 144.2 %copy-start.15 = (bf16[6144]{0:T(1024)(128)(2,1)S(1)}, bf16[6144]{0:T(1024)(128)(2,1)}, u32[]{:S(2)}) copy-start(bf16[6144]{0:T(1024)(128)(2,1)} %param.27) | copy-start | bytes 36868
  373.6 123.7 %copy-start.1 = (bf16[6144,64]{0,1:T(8,128)(2,1)S(1)}, bf16[6144,64]{0,1:T(8,128)(2,1)}, u32[]{:S(2)}) copy-start(bf16[6144,64]{0,1:T(8,128)(2,1)} %param.24) | copy-start | bytes 2359300
  375.4 121.9 %copy-start.10 = (bf16[960,384]{1,0:T(8,128)(2,1)}, bf16[960,384]{1,0:T(8,128)(2,1)S(1)}, u32[]{:S(2)}) copy-start(bf16[960,384]{1,0:T(8,128)(2,1)S(1)} %add_convert_fusion) | copy-start | bytes 2211844
  391.8 9.5 %collective-permute-start.2 = (bf16[2,6144]{1,0:T(2,128)(2,1)S(1)}, bf16[2,6144]{1,0:T(2,128)(2,1)S(1)}, u32[]{:S(2)}, u32[]{:S(2)}) collective-permute-start(bf16[2,6144]{1,0:T(2,128)(2,1)S(1)} %all_gather.11), channel_id=1, source_target_pairs={{0,16},{16,32},{32,48},{48,64},{64,80},{80,96},{96,112},{112,0},{1... | collective-permute-start | bytes 73736 | tf_op jit(solution)/shard_map/ppermute | solution.py:141
  401.3 3.3 collective-permute-start.3
  404.5 4.3 collective-permute-start.4
  408.9 4.5 collective-permute-start.5
  413.3 4.5 collective-permute-start.6
  417.8 4.5 collective-permute-start.7
  422.2 4.5 collective-permute-start.8
Sparse Core Ops, SparseCore 0:
  26.2 63.1 all-gather.2
  112.3 94.4 all-gather.4
  278.2 95.3 reduce-scatter.3
